TPU v7x, 128 devices: a whole 4x4x4 slice. The times are simulated.
128 devices in a mesh: ray: 16 (over x, z), tile: 8 (over y, core).
Axes of the slice: x: 4, y: 4, z: 4, core: 2. Of those that a mesh axis runs over, the one named last changes fastest.
Arguments:
- data: float32 [64, 262144], P(None, ('ray', 'tile')), may hold values from -6 to 6
- sensitivity: bfloat16 [4096, 256, 512], P(('ray', 'tile')), may hold values from -0.25 to 0.25
- block_tiles: int32 [128, 8, 4], P(('ray', 'tile')), may hold values from 0 to 47
- block_bundles: int32 [128, 8, 4], P(('ray', 'tile')), may hold values from 0 to 7
Outputs:
- solution: float32 [64, 196608], P(None, 'tile')
- residual: float32 [64, 262144], P(None, ('ray', 'tile'))
Inputs may be any that keep to these rules, and one draw needn't show every extreme that they name: `block_tiles`: position of the block's tile among the 48 tiles of the owner given by the second index. `block_bundles`: the block's ray bundle among the device's 8 bundles.
All inputs are finite; a program needn't handle non-finite values.
Results may differ from a plain program's by a relative error of at most 0.004.
The roundings to bfloat16 on the way count: a program that leaves them out, or rounds other values in their place, can miss the bound.
Values may be sent and summed in bfloat16 or wider, within the bound.
A program may use at most 128 MiB of HBM per device.

v0:
```python
import jax
import jax.numpy as jnp
from jax import lax
from jax.sharding import PartitionSpec as P

RB = 256
CB = 512
ITERS = 2
BUND_DEV = 8
TILE_DEV = 48
eps_norm = 1e-06


def per_device(data, sensitivity, block_tiles, block_bundles):
    columns = data.shape[0]
    bundles = block_bundles.reshape(-1)
    requests = lax.all_to_all(block_tiles, "tile", split_axis=1, concat_axis=1, tiled=True).reshape(
        -1
    )
    bundle_onehot = (bundles[:, None] == jnp.arange(BUND_DEV, dtype=jnp.int32)[None, :]).astype(
        jnp.float32
    )
    owner_onehot = (requests[:, None] == jnp.arange(TILE_DEV, dtype=jnp.int32)[None, :]).astype(
        jnp.bfloat16
    )

    def fetch(field_bf):
        owned = field_bf.reshape(columns, TILE_DEV, CB)
        outgoing = jnp.take(owned, requests, axis=1)
        tiles = lax.all_to_all(outgoing, "tile", split_axis=1, concat_axis=1, tiled=True)
        return tiles

    def forward(field_bf):
        tiles = fetch(field_bf)
        partial_value = jnp.einsum(
            "cnk,nrk->ncr", tiles, sensitivity, preferred_element_type=jnp.float32
        )
        summed = jnp.einsum(
            "ncr,nb->cbr", partial_value, bundle_onehot, precision=lax.Precision.HIGHEST
        )
        return summed.reshape(columns, BUND_DEV * RB)

    def adjoint(rays_bf):
        picked = jnp.take(rays_bf.reshape(columns, BUND_DEV, RB), bundles, axis=1)
        terms = jnp.einsum(
            "cnr,nrk->cnk", picked, sensitivity, preferred_element_type=jnp.float32
        ).astype(jnp.bfloat16)
        arrived = lax.all_to_all(terms, "tile", split_axis=1, concat_axis=1, tiled=True)
        owned = jnp.einsum(
            "cnk,nt->ctk", arrived, owner_onehot, preferred_element_type=jnp.float32
        ).reshape(columns, TILE_DEV * CB)
        total = lax.psum(owned, "ray")
        return total

    def cell_norm(field):
        local = jnp.sum(field * field, axis=1)
        total = lax.psum(local, "tile")
        return jnp.sqrt(total + eps_norm)

    def ray_norm(rays):
        total = lax.psum(jnp.sum(rays * rays, axis=1), ("ray", "tile"))
        return jnp.sqrt(total + eps_norm)

    beta_now = ray_norm(data)
    rays_dir = data / beta_now[:, None]
    model_dir = adjoint(rays_dir.astype(jnp.bfloat16))
    alpha_now = cell_norm(model_dir)
    model_dir = model_dir / alpha_now[:, None]
    search = model_dir
    solution = jnp.zeros_like(model_dir)
    phi_bar = beta_now
    rho_bar = alpha_now
    for step in range(ITERS):
        rounded = model_dir.astype(jnp.bfloat16)
        rays_dir = forward(rounded) - alpha_now[:, None] * rays_dir
        beta_now = ray_norm(rays_dir)
        rays_dir = rays_dir / beta_now[:, None]
        rho_now = jnp.sqrt(rho_bar * rho_bar + beta_now * beta_now)
        cosine = rho_bar / rho_now
        sine_part = beta_now / rho_now
        phi_now = cosine * phi_bar
        phi_bar = sine_part * phi_bar
        solution = solution + (phi_now / rho_now)[:, None] * search
        if step + 1 < ITERS:
            model_dir = adjoint(rays_dir.astype(jnp.bfloat16)) - beta_now[:, None] * model_dir
            alpha_now = cell_norm(model_dir)
            model_dir = model_dir / alpha_now[:, None]
            theta_now = sine_part * alpha_now
            rho_bar = -cosine * alpha_now
            search = model_dir - (theta_now / rho_now)[:, None] * search
    residual = data - forward(solution.astype(jnp.bfloat16))
    return (solution, residual)


def solution(mesh):
    return jax.shard_map(
        per_device,
        mesh=mesh,
        in_specs=(
            P(None, ("ray", "tile")),
            P(("ray", "tile"), None, None),
            P(("ray", "tile"), None, None),
            P(("ray", "tile"), None, None),
        ),
        out_specs=(P(None, "tile"), P(None, ("ray", "tile"))),
        check_vma=False,
    )
```

profile of v0, /device:TPU:1, one launch (start us, length us, event | category | flops | bytes accessed | tf_op | source)
XLA Modules:
  0.0 731.6 jit_solution(17410393598439722855)
XLA Ops:
  8.5 6.0 all-to-all-start
  16.5 67.7 %psum.49 = f32[64]{0:T(128)S(1)} all-reduce(f32[64]{0:T(128)S(1)} %multiply_reduce_fusion.4), channel_id=1, replica_groups=mesh['ray'=16,'tile'=8] {'ray','tile'}, use_global_device_ids=true, to_apply=%region_1.0 | all-reduce | flops 64 | bytes 512 | tf_op jit(solution)/shard_map/psum | solution.py:61
  86.1 6.3 convert_bitcast_fusion.1
  92.4 4.4 all-to-all-start.1
  98.1 25.1 %all-to-all-done.1 = bf16[64,32,512]{2,0,1:T(8,128)(2,1)S(1)} async-done(((bf16[64,32,512]{2,0,1:T(8,128)(2,1)}), bf16[64,32,512]{2,0,1:T(8,128)(2,1)S(1)}, u32[]{:S(2)}, u32[]{:S(2)}) %all-to-all-start.1) | async-done | bytes 2097184 | tf_op jit(solution)/shard_map/all_to_all | solution.py:48
  124.9 6.3 copy.39
  131.3 119.1 %all-reduce.3.cloned.1.call-done = f32[64,24576]{1,0:T(8,128)} async-done(((f32[64,24576]{1,0:T(8,128)}), f32[64,24576]{1,0:T(8,128)}) %all-reduce.3.cloned.1.call-update) | async-done | bytes 6291472 | tf_op jit(solution)/shard_map/psum | solution.py:52
  250.4 3.3 multiply_reduce_fusion.1
  253.7 12.4 %psum.51 = f32[64]{0:T(128)S(1)} all-reduce(f32[64]{0:T(128)S(1)} %multiply_reduce_fusion.1), channel_id=1, replica_groups=mesh['ray'=16,'tile'=8] {'tile'}, use_global_device_ids=true, to_apply=%region_4.6 | all-reduce | flops 64 | bytes 512 | tf_op jit(solution)/shard_map/psum | solution.py:57
  266.1 3.2 fusion.37
  269.8 2.0 gather_fusion.1
  273.7 31.7 %all_to_all.30 = bf16[64,32,512]{2,0,1:T(8,128)(2,1)S(1)} all-to-all(bf16[64,32,512]{2,0,1:T(8,128)(2,1)S(1)} %select_bitcast_fusion.2), channel_id=1, replica_groups=mesh['ray'=16,'tile'=8] {'tile'}, dimensions={1} | all-to-all | bytes 4194304 | tf_op jit(solution)/shard_map/all_to_all | solution.py:30
  305.4 6.0 fusion.41
  311.5 2.0 fusion.6
  313.9 64.5 %psum.52 = f32[64]{0:T(128)S(1)} all-reduce(f32[64]{0:T(128)S(1)} %get-tuple-element.11), channel_id=1, replica_groups=mesh['ray'=16,'tile'=8] {'ray','tile'}, use_global_device_ids=true, to_apply=%region_6.0 | all-reduce | flops 64 | bytes 512 | tf_op jit(solution)/shard_map/psum | solution.py:61
  379.2 5.0 convert_bitcast_fusion
  384.2 30.1 %all_to_all.31 = bf16[64,32,512]{2,0,1:T(8,128)(2,1)S(1)} all-to-all(bf16[64,32,512]{2,0,1:T(8,128)(2,1)S(1)} %convert_bitcast_fusion), channel_id=1, replica_groups=mesh['ray'=16,'tile'=8] {'tile'}, dimensions={1} | all-to-all | bytes 4194304 | tf_op jit(solution)/shard_map/all_to_all | solution.py:48
  416.0 6.3 copy.41
  422.3 118.9 %all-reduce.5.cloned.1.call-done = f32[64,24576]{1,0:T(8,128)} async-done(((f32[64,24576]{1,0:T(8,128)}), f32[64,24576]{1,0:T(8,128)}) %all-reduce.5.cloned.1.call-update) | async-done | bytes 6291472 | tf_op jit(solution)/shard_map/psum | solution.py:52
  541.2 5.8 multiply_reduce_fusion
  547.0 12.4 %psum.54 = f32[64]{0:T(128)S(1)} all-reduce(f32[64]{0:T(128)S(1)} %multiply_reduce_fusion), channel_id=1, replica_groups=mesh['ray'=16,'tile'=8] {'tile'}, use_global_device_ids=true, to_apply=%region_9.12 | all-reduce | flops 64 | bytes 512 | tf_op jit(solution)/shard_map/psum | solution.py:57
  559.4 5.2 fusion.10
  565.1 2.0 gather_fusion.3
  568.9 31.7 %all_to_all.32 = bf16[64,32,512]{2,0,1:T(8,128)(2,1)S(1)} all-to-all(bf16[64,32,512]{2,0,1:T(8,128)(2,1)S(1)} %select_bitcast_fusion.1), channel_id=1, replica_groups=mesh['ray'=16,'tile'=8] {'tile'}, dimensions={1} | all-to-all | bytes 4194304 | tf_op jit(solution)/shard_map/all_to_all | solution.py:30
  600.7 6.0 fusion.42
  606.7 2.0 fusion.2
  609.1 64.8 %psum.55 = f32[64]{0:T(128)S(1)} all-reduce(f32[64]{0:T(128)S(1)} %multiply_reduce_fusion.2), channel_id=1, replica_groups=mesh['ray'=16,'tile'=8] {'ray','tile'}, use_global_device_ids=true, to_apply=%region_11.14 | all-reduce | flops 64 | bytes 512 | tf_op jit(solution)/shard_map/psum | solution.py:61
  673.9 7.4 %fusion.38 = (bf16[64,24576]{1,0:T(8,128)(2,1)S(1)}, f32[64,24576]{1,0:T(8,128)}) fusion(f32[64]{0:T(128)S(1)} %multiply_divide_fusion, f32[64]{0:T(128)S(1)} %add_sqrt_fusion, f32[64,24576]{1,0:T(8,128)} %all-reduce.5.cloned.1.call-done, f32[64]{0:T(128)S(1)} %get-tuple-element.13, f32[64]{0:T(128)S(1)} %get-tuple-element.9, ...), kind=kLoop, calls=%fused_computation.76 | loop fusion | flops 15728640 | bytes 22021632 | tf_op jit(solution)/shard_map/convert_element_type | solution.py:91
  681.7 2.0 gather_fusion.4
  685.6 30.1 %all_to_all.33 = bf16[64,32,512]{2,0,1:T(8,128)(2,1)S(1)} all-to-all(bf16[64,32,512]{2,0,1:T(8,128)(2,1)S(1)} %select_bitcast_fusion), channel_id=1, replica_groups=mesh['ray'=16,'tile'=8] {'tile'}, dimensions={1} | all-to-all | bytes 4194304 | tf_op jit(solution)/shard_map/all_to_all | solution.py:30
  715.7 6.0 fusion.43
  721.8 2.0 fusion
  (52 shorter events, 19.5 us)
Async XLA Ops:
  8.5 83.9 %all-to-all-start = ((s32[1,8,4]{2,0,1:T(1,128)}), s32[1,8,4]{2,0,1:T(1,128)S(1)}, u32[]{:S(2)}, u32[]{:S(2)}) async-start(s32[1,8,4]{2,0,1:T(1,128)} %copy.22), calls=%async_computation | async-start | bytes 8192 | tf_op jit(solution)/shard_map/all_to_all | solution.py:17
  92.4 30.8 %all-to-all-start.1 = ((bf16[64,32,512]{2,0,1:T(8,128)(2,1)}), bf16[64,32,512]{2,0,1:T(8,128)(2,1)S(1)}, u32[]{:S(2)}, u32[]{:S(2)}) async-start(bf16[64,32,512]{2,0,1:T(8,128)(2,1)} %convert_bitcast_fusion.1), calls=%async_computation.1 | async-start | bytes 4194304 | tf_op jit(solution)/shard_map/all_to_all | solution.py:48
  96.8 153.6 %all-reduce.3.cloned.1.call-start = ((), (), s32[]{:S(2)}) async-start(), calls=%async_computation.6 | async-start | bytes 12582912 | tf_op jit(solution)/shard_map/psum | solution.py:52
  131.2 410.0 %all-reduce.5.cloned.1.call-start = ((), (), s32[]{:S(2)}) async-start(), calls=%async_computation.7 | async-start | bytes 12582912 | tf_op jit(solution)/shard_map/psum | solution.py:52
  311.4 2.1 copy-start
  313.9 64.7 %copy-start.2 = (f32[64,2048]{1,0:T(8,128)}, f32[64,2048]{1,0:T(8,128)S(1)}, u32[]{:S(2)}) copy-start(f32[64,2048]{1,0:T(8,128)S(1)} %get-tuple-element.12) | copy-start | bytes 1572868
  606.7 2.1 copy-start.3
  721.7 2.1 copy-start.1
Sparse Core Ops, SparseCore 0:
  131.3 119.0 all-reduce.2
  422.4 118.6 all-reduce.4
where the time goes:
time: 733 us; the launch traced here: 732 us
  blocking collectives  346 us (47%)
  waiting for transfers between devices  263 us (36%)
  matrix products  38.8 us (5%)
  other arithmetic  35 us (5%)
  local copies, waits for them, and re-layouts  24.4 us (3%)
  between operations  14.3 us (2%)
  starting transfers between devices  10.4 us (1%)
    psum x2, waiting for transfers between devices, adjoint(): total = lax.psum(owned, 'ray')  238 us
    psum x3, blocking collectives, ray_norm(): total = lax.psum(jnp.sum(rays * rays, axis=1), ('ray', 'tile'))  197 us
    all_to_all x3, blocking collectives, fetch(): lax.all_to_all(outgoing, 'tile', split_axis=1, concat_axis=1, tiled=True)  93.6 us
    all_to_all x1, blocking collectives, adjoint(): lax.all_to_all(terms, 'tile', split_axis=1, concat_axis=1, tiled=True)  30.1 us
    all_to_all x1, waiting for transfers between devices, adjoint(): lax.all_to_all(terms, 'tile', split_axis=1, concat_axis=1, tiled=True)  25.1 us
    psum x2, blocking collectives, cell_norm(): total = lax.psum(local, 'tile')  24.9 us
    dot_general x3, matrix products, forward(): jnp.einsum('cnk,nrk->ncr', tiles, sensitivity, preferred_element_type=jnp...  18.1 us
    unnamed x15, local copies, waits for them, and re-layouts  15.1 us
  transfers between devices with their start and end apart: 4, of which 3 were waited for; matrix products, arithmetic and copies ran while one was open for 2% of the time, Pallas kernels for 0%

commit v1 on v0

--- a/solution.py
+++ b/solution.py
@@ -58,7 +58,8 @@
         return jnp.sqrt(total + eps_norm)
 
     def ray_norm(rays):
-        total = lax.psum(jnp.sum(rays * rays, axis=1), ("ray", "tile"))
+        original = jnp.sum(rays * rays, axis=1)
+        total = lax.psum(lax.psum(original, axis_name="tile"), "ray")
         return jnp.sqrt(total + eps_norm)
 
     beta_now = ray_norm(data)

time: 733 us -> 690 us (0.941)
  blocking collectives: 346 us -> 297 us
  starting transfers between devices: 10.4 us -> 19.9 us
    psum x3 -> x6, blocking collectives: 197 us -> 134 us  [ray_norm(): total = lax.psum(lax.psum(original, axis_name='tile'), 'ray')]
    all_to_all x1, starting transfers between devices: 4.4 us -> 13.9 us  [adjoint(): lax.all_to_all(terms, 'tile', split_axis=1, concat_axis=1, tiled=True)]
where the time goes in v1:
time: 690 us; the launch traced here: 689 us
  blocking collectives  297 us (43%)
  waiting for transfers between devices  260 us (38%)
  matrix products  38.8 us (6%)
  other arithmetic  35 us (5%)
  local copies, waits for them, and re-layouts  24.3 us (4%)
  starting transfers between devices  19.9 us (3%)
  between operations  14.3 us (2%)
    psum x2, waiting for transfers between devices, adjoint(): total = lax.psum(owned, 'ray')  234 us
    psum x6, blocking collectives, ray_norm(): total = lax.psum(lax.psum(original, axis_name='tile'), 'ray')  134 us
    all_to_all x3, blocking collectives, fetch(): lax.all_to_all(outgoing, 'tile', split_axis=1, concat_axis=1, tiled=True)  100 us
    all_to_all x1, blocking collectives, adjoint(): lax.all_to_all(terms, 'tile', split_axis=1, concat_axis=1, tiled=True)  37 us
    psum x2, blocking collectives, cell_norm(): total = lax.psum(local, 'tile')  25.1 us
    all_to_all x1, waiting for transfers between devices, adjoint(): lax.all_to_all(terms, 'tile', split_axis=1, concat_axis=1, tiled=True)  25.1 us
    dot_general x3, matrix products, forward(): jnp.einsum('cnk,nrk->ncr', tiles, sensitivity, preferred_element_type=jnp...  18.1 us
    unnamed x15, local copies, waits for them, and re-layouts  15.1 us
  transfers between devices with their start and end apart: 4, of which 3 were waited for; matrix products, arithmetic and copies ran while one was open for 2% of the time, Pallas kernels for 0%

profile of v1, /device:TPU:1, one launch (start us, length us, event | category | flops | bytes accessed | tf_op | source)
XLA Modules:
  0.0 689.0 jit_solution(5747341820461819291)
XLA Ops:
  8.5 6.0 all-to-all-start
  16.5 12.2 %psum.70 = f32[64]{0:T(128)S(1)} all-reduce(f32[64]{0:T(128)S(1)} %multiply_reduce_fusion.4), channel_id=1, replica_groups=mesh['ray'=16,'tile'=8] {'tile'}, use_global_device_ids=true, to_apply=%region_1.0 | all-reduce | flops 64 | bytes 512 | tf_op jit(solution)/shard_map/psum | solution.py:62
  28.7 34.5 %psum.71 = f32[64]{0:T(128)S(1)} all-reduce(f32[64]{0:T(128)S(1)} %psum.70), channel_id=1, replica_groups=mesh['ray'=16,'tile'=8] {'ray'}, use_global_device_ids=true, to_apply=%region_2.0 | all-reduce | flops 64 | bytes 512 | tf_op jit(solution)/shard_map/psum | solution.py:62
  65.0 6.3 convert_bitcast_fusion.1
  71.3 13.9 %all-to-all-start.1 = ((bf16[64,32,512]{2,0,1:T(8,128)(2,1)}), bf16[64,32,512]{2,0,1:T(8,128)(2,1)S(1)}, u32[]{:S(2)}, u32[]{:S(2)}) async-start(bf16[64,32,512]{2,0,1:T(8,128)(2,1)} %convert_bitcast_fusion.1), calls=%async_computation.1 | async-start | bytes 4194304 | tf_op jit(solution)/shard_map/all_to_all | solution.py:48
  86.5 25.1 %all-to-all-done.1 = bf16[64,32,512]{2,0,1:T(8,128)(2,1)S(1)} async-done(((bf16[64,32,512]{2,0,1:T(8,128)(2,1)}), bf16[64,32,512]{2,0,1:T(8,128)(2,1)S(1)}, u32[]{:S(2)}, u32[]{:S(2)}) %all-to-all-start.1) | async-done | bytes 2097184 | tf_op jit(solution)/shard_map/all_to_all | solution.py:48
  113.3 6.3 copy.39
  119.7 117.1 %all-reduce.3.cloned.1.call-done = f32[64,24576]{1,0:T(8,128)} async-done(((f32[64,24576]{1,0:T(8,128)}), f32[64,24576]{1,0:T(8,128)}) %all-reduce.3.cloned.1.call-update) | async-done | bytes 6291472 | tf_op jit(solution)/shard_map/psum | solution.py:52
  236.8 3.3 multiply_reduce_fusion.1
  240.1 12.4 %psum.73 = f32[64]{0:T(128)S(1)} all-reduce(f32[64]{0:T(128)S(1)} %multiply_reduce_fusion.1), channel_id=1, replica_groups=mesh['ray'=16,'tile'=8] {'tile'}, use_global_device_ids=true, to_apply=%region_5.7 | all-reduce | flops 64 | bytes 512 | tf_op jit(solution)/shard_map/psum | solution.py:57
  252.6 3.2 fusion.37
  256.2 2.0 gather_fusion.1
  260.1 31.7 %all_to_all.30 = bf16[64,32,512]{2,0,1:T(8,128)(2,1)S(1)} all-to-all(bf16[64,32,512]{2,0,1:T(8,128)(2,1)S(1)} %select_bitcast_fusion.2), channel_id=1, replica_groups=mesh['ray'=16,'tile'=8] {'tile'}, dimensions={1} | all-to-all | bytes 4194304 | tf_op jit(solution)/shard_map/all_to_all | solution.py:30
  291.8 6.0 fusion.41
  300.3 12.8 %psum.74 = f32[64]{0:T(128)S(1)} all-reduce(f32[64]{0:T(128)S(1)} %get-tuple-element.11), channel_id=1, replica_groups=mesh['ray'=16,'tile'=8] {'tile'}, use_global_device_ids=true, to_apply=%region_7.0 | all-reduce | flops 64 | bytes 512 | tf_op jit(solution)/shard_map/psum | solution.py:62
  313.1 31.1 %psum.75 = f32[64]{0:T(128)S(1)} all-reduce(f32[64]{0:T(128)S(1)} %psum.74), channel_id=1, replica_groups=mesh['ray'=16,'tile'=8] {'ray'}, use_global_device_ids=true, to_apply=%region_8.11 | all-reduce | flops 64 | bytes 512 | tf_op jit(solution)/shard_map/psum | solution.py:62
  345.0 5.0 convert_bitcast_fusion
  350.0 37.0 %all_to_all.31 = bf16[64,32,512]{2,0,1:T(8,128)(2,1)S(1)} all-to-all(bf16[64,32,512]{2,0,1:T(8,128)(2,1)S(1)} %convert_bitcast_fusion), channel_id=1, replica_groups=mesh['ray'=16,'tile'=8] {'tile'}, dimensions={1} | all-to-all | bytes 4194304 | tf_op jit(solution)/shard_map/all_to_all | solution.py:48
  388.7 6.3 copy.41
  395.0 117.3 %all-reduce.5.cloned.1.call-done = f32[64,24576]{1,0:T(8,128)} async-done(((f32[64,24576]{1,0:T(8,128)}), f32[64,24576]{1,0:T(8,128)}) %all-reduce.5.cloned.1.call-update) | async-done | bytes 6291472 | tf_op jit(solution)/shard_map/psum | solution.py:52
  512.3 5.8 multiply_reduce_fusion
  518.1 12.7 %psum.77 = f32[64]{0:T(128)S(1)} all-reduce(f32[64]{0:T(128)S(1)} %multiply_reduce_fusion), channel_id=1, replica_groups=mesh['ray'=16,'tile'=8] {'tile'}, use_global_device_ids=true, to_apply=%region_11.14 | all-reduce | flops 64 | bytes 512 | tf_op jit(solution)/shard_map/psum | solution.py:57
  530.8 5.2 fusion.10
  536.4 2.0 gather_fusion.3
  540.3 31.7 %all_to_all.32 = bf16[64,32,512]{2,0,1:T(8,128)(2,1)S(1)} all-to-all(bf16[64,32,512]{2,0,1:T(8,128)(2,1)S(1)} %select_bitcast_fusion.1), channel_id=1, replica_groups=mesh['ray'=16,'tile'=8] {'tile'}, dimensions={1} | all-to-all | bytes 4194304 | tf_op jit(solution)/shard_map/all_to_all | solution.py:30
  572.0 6.0 fusion.42
  580.5 12.8 %psum.78 = f32[64]{0:T(128)S(1)} all-reduce(f32[64]{0:T(128)S(1)} %multiply_reduce_fusion.2), channel_id=1, replica_groups=mesh['ray'=16,'tile'=8] {'tile'}, use_global_device_ids=true, to_apply=%region_13.16 | all-reduce | flops 64 | bytes 512 | tf_op jit(solution)/shard_map/psum | solution.py:62
  593.3 31.1 %psum.79 = f32[64]{0:T(128)S(1)} all-reduce(f32[64]{0:T(128)S(1)} %psum.78), channel_id=1, replica_groups=mesh['ray'=16,'tile'=8] {'ray'}, use_global_device_ids=true, to_apply=%region_14.17 | all-reduce | flops 64 | bytes 512 | tf_op jit(solution)/shard_map/psum | solution.py:62
  624.4 7.4 %fusion.38 = (bf16[64,24576]{1,0:T(8,128)(2,1)S(1)}, f32[64,24576]{1,0:T(8,128)}) fusion(f32[64]{0:T(128)S(1)} %multiply_divide_fusion, f32[64]{0:T(128)S(1)} %add_sqrt_fusion, f32[64,24576]{1,0:T(8,128)} %all-reduce.5.cloned.1.call-done, f32[64]{0:T(128)S(1)} %get-tuple-element.13, f32[64]{0:T(128)S(1)} %get-tuple-element.9, ...), kind=kLoop, calls=%fused_computation.76 | loop fusion | flops 15728640 | bytes 22021632 | tf_op jit(solution)/shard_map/convert_element_type | solution.py:92
  632.2 2.0 gather_fusion.4
  636.1 37.0 %all_to_all.33 = bf16[64,32,512]{2,0,1:T(8,128)(2,1)S(1)} all-to-all(bf16[64,32,512]{2,0,1:T(8,128)(2,1)S(1)} %select_bitcast_fusion), channel_id=1, replica_groups=mesh['ray'=16,'tile'=8] {'tile'}, dimensions={1} | all-to-all | bytes 4194304 | tf_op jit(solution)/shard_map/all_to_all | solution.py:30
  673.0 6.0 fusion.43
  (55 shorter events, 25.4 us)
Async XLA Ops:
  8.5 62.8 %all-to-all-start = ((s32[1,8,4]{2,0,1:T(1,128)}), s32[1,8,4]{2,0,1:T(1,128)S(1)}, u32[]{:S(2)}, u32[]{:S(2)}) async-start(s32[1,8,4]{2,0,1:T(1,128)} %copy.22), calls=%async_computation | async-start | bytes 8192 | tf_op jit(solution)/shard_map/all_to_all | solution.py:17
  71.3 40.3 %all-to-all-start.1 = ((bf16[64,32,512]{2,0,1:T(8,128)(2,1)}), bf16[64,32,512]{2,0,1:T(8,128)(2,1)S(1)}, u32[]{:S(2)}, u32[]{:S(2)}) async-start(bf16[64,32,512]{2,0,1:T(8,128)(2,1)} %convert_bitcast_fusion.1), calls=%async_computation.1 | async-start | bytes 4194304 | tf_op jit(solution)/shard_map/all_to_all | solution.py:48
  85.2 151.6 %all-reduce.3.cloned.1.call-start = ((), (), s32[]{:S(2)}) async-start(), calls=%async_computation.6 | async-start | bytes 12582912 | tf_op jit(solution)/shard_map/psum | solution.py:52
  119.6 392.7 %all-reduce.5.cloned.1.call-start = ((), (), s32[]{:S(2)}) async-start(), calls=%async_computation.7 | async-start | bytes 12582912 | tf_op jit(solution)/shard_map/psum | solution.py:52
  297.9 2.1 copy-start
  300.3 44.1 %copy-start.2 = (f32[64,2048]{1,0:T(8,128)}, f32[64,2048]{1,0:T(8,128)S(1)}, u32[]{:S(2)}) copy-start(f32[64,2048]{1,0:T(8,128)S(1)} %get-tuple-element.12) | copy-start | bytes 1572868
  578.1 2.1 copy-start.3
  679.1 2.1 copy-start.1
Sparse Core Ops, SparseCore 0:
  119.7 117.0 all-reduce.2
  395.1 117.1 all-reduce.4
